TPU v7x, 32 devices: a whole 2x2x4 slice. The times are simulated.
32 devices in a mesh: tok: 8 (over z, x), head: 4 (over y, core).
Axes of the slice: x: 2, y: 2, z: 4, core: 2. Of those that a mesh axis runs over, the one named last changes fastest.
Arguments:
- queries: bfloat16 [2048, 3072], P('tok', 'head'), may hold values from -96 to 96
- key_rows: bfloat16 [2048, 512], P('tok', 'head'), may hold values from -6 to 6
- value_rows: bfloat16 [2048, 512], P('tok', 'head'), may hold values from -12 to 12
- tile_mask: int32 [16, 16], P('tok'), may hold values from 0 to 1, as said below
- out_weight: bfloat16 [3072, 6144], P('head'), may hold values from -0.109375 to 0.109375
Outputs:
- mixed: bfloat16 [2048, 6144], P('tok', 'head')
Inputs may be any that keep to these rules, and one draw needn't show every extreme that they name: `tile_mask`: row r keeps key tile r; every row keeps between 1 and 8 tiles, and some row keeps exactly 8.
All inputs are finite; a program needn't handle non-finite values.
Results may differ from a plain program's by a relative error of at most 0.012.
Values may be sent and summed in bfloat16 or wider, within the bound.
A program may use at most 128 MiB of HBM per device.

v0:
```python
import math
import jax
import jax.numpy as jnp
from jax import lax
from jax.sharding import PartitionSpec as P

HD = 128
TILE = 128
NEGATIVE = -1e30
tiles_per_turn = 16


def tile_block(query_tile, key_chosen, value_chosen, shown_tiles, state, score_scale):
    scores = (
        jnp.einsum("qgjd,ckgd->gjqck", query_tile, key_chosen, preferred_element_type=jnp.float32)
        * score_scale
    )
    shown = shown_tiles[None, None, None, :]
    tile_max = jnp.where(shown, jnp.max(scores, axis=-1), NEGATIVE)
    prob_bf = jnp.where(shown[..., None], jnp.exp(scores - tile_max[..., None]), 0.0).astype(
        jnp.bfloat16
    )
    tile_sums = jnp.sum(prob_bf.astype(jnp.float32), axis=-1)
    tile_parts = jnp.einsum(
        "gjqck,ckgd->gjqcd", prob_bf, value_chosen, preferred_element_type=jnp.float32
    )
    running_max, denominator, numerator = state
    new_max = jnp.maximum(running_max, jnp.max(tile_max, axis=-1))
    rescale = jnp.exp(running_max - new_max)
    tile_weight = jnp.where(shown, jnp.exp(tile_max - new_max[..., None]), 0.0)
    denominator = denominator * rescale + jnp.sum(tile_weight * tile_sums, axis=-1)
    numerator = numerator * rescale[..., None] + jnp.sum(
        tile_weight[..., None] * tile_parts, axis=3
    )
    return (new_max, denominator, numerator)


def sweep_piece(state, query_tile, living, key_tiles, value_tiles, score_scale):
    tile_count = living.shape[0]
    block_tiles = min(tiles_per_turn, tile_count)
    ordering = jnp.argsort(1 - living, stable=True)
    live_total = jnp.sum(living)
    turn_count = (live_total + block_tiles - 1) // block_tiles

    def one_turn(turn_index, inner):
        offset = turn_index * block_tiles
        picked = lax.dynamic_slice_in_dim(ordering, offset, block_tiles)
        shown_tiles = offset + jnp.arange(block_tiles, dtype=jnp.int32) < live_total
        return tile_block(
            query_tile,
            jnp.take(key_tiles, picked, axis=0),
            jnp.take(value_tiles, picked, axis=0),
            shown_tiles,
            inner,
            score_scale,
        )

    return lax.fori_loop(0, turn_count, one_turn, state)


def per_device(queries, key_rows, value_rows, tile_mask, out_weight):
    own_rows = queries.shape[0]
    local_heads = queries.shape[1]
    slot_total = own_rows // TILE
    kv_local = key_rows.shape[1] // HD
    group_size = local_heads // HD // kv_local
    score_scale = 1.0 / math.sqrt(HD)
    query_tiles = queries.reshape(slot_total, TILE, kv_local, group_size, HD)
    slot_rows = [tile_mask[number] for number in range(slot_total)]
    slot_queries = [query_tiles[number] for number in range(slot_total)]
    slot_active = [jnp.int32(1) for number in range(slot_total)]
    empty_max = jnp.full((kv_local, group_size, TILE), NEGATIVE, jnp.float32)
    empty_sum = jnp.zeros((kv_local, group_size, TILE), jnp.float32)
    empty_out = jnp.zeros((kv_local, group_size, TILE, HD), jnp.float32)
    initial = tuple(((empty_max, empty_sum, empty_out) for number in range(len(slot_rows))))
    every_key, every_value = (
        lax.all_gather(key_rows, "tok", axis=0, tiled=True),
        lax.all_gather(value_rows, "tok", axis=0, tiled=True),
    )
    tile_count = every_key.shape[0] // TILE
    key_tiles = every_key.reshape(tile_count, TILE, kv_local, HD)
    value_tiles = every_value.reshape(tile_count, TILE, kv_local, HD)
    result = []
    for absorb_number in range(len(slot_rows)):
        living = slot_rows[absorb_number] * slot_active[absorb_number]
        result.append(
            sweep_piece(
                initial[absorb_number],
                slot_queries[absorb_number],
                living,
                key_tiles,
                value_tiles,
                score_scale,
            )
        )
    carries = tuple(result)
    finished = []
    for number in range(len(slot_rows)):
        running_max, denominator, numerator = carries[number]
        safe_sum = jnp.where(denominator > 0, denominator, 1.0)
        attended = numerator / safe_sum[..., None]
        finished.append(
            attended.transpose(2, 0, 1, 3).reshape(TILE, local_heads).astype(jnp.bfloat16)
        )
    own_stack = jnp.stack(finished[:slot_total])
    attention = own_stack.reshape(own_rows, local_heads)
    mixed = lax.psum_scatter(
        lax.dot_general(
            out_weight, attention, (((0,), (1,)), ((), ())), preferred_element_type=jnp.float32
        ).astype(jnp.bfloat16),
        "head",
        scatter_dimension=0,
        tiled=True,
    )
    return mixed.T


def solution(mesh):
    return jax.shard_map(
        per_device,
        mesh=mesh,
        in_specs=(
            P("tok", "head"),
            P("tok", "head"),
            P("tok", "head"),
            P("tok", None),
            P("head", None),
        ),
        out_specs=P("tok", "head"),
        check_vma=False,
    )
```

profile of v0, /device:TPU:0, one launch (start us, length us, event | category | flops | bytes accessed | tf_op | source)
XLA Modules:
  0.0 161.2 jit_solution(17541276726180953449)
XLA Ops:
  6.5 1.4 subtract_bitcast_fusion.1
  8.6 1.3 sort.32
  10.5 1.3 sort.31
  11.9 33.3 %all_gather.7 = bf16[2048,128]{1,0:T(8,128)(2,1)S(1)} all-gather(bf16[256,128]{1,0:T(8,128)(2,1)} %param.13), channel_id=1, replica_groups=mesh['tok'=8,'head'=4] {'tok'}, dimensions={0}, use_global_device_ids=true | all-gather | bytes 589824 | tf_op jit(solution)/shard_map/all_gather | solution.py:78
  45.1 31.4 %all_gather.6 = bf16[2048,128]{1,0:T(8,128)(2,1)S(1)} all-gather(bf16[256,128]{1,0:T(8,128)(2,1)} %param.12), channel_id=1, replica_groups=mesh['tok'=8,'head'=4] {'tok'}, dimensions={0}, use_global_device_ids=true | all-gather | bytes 589824 | tf_op jit(solution)/shard_map/all_gather | solution.py:77
  76.5 0.6 gather_fusion.3
  77.2 0.6 gather_fusion.2
  77.9 0.6 gather_fusion.1
  78.5 0.6 gather_fusion
  79.2 1.1 fusion.37
  80.8 12.8 %while.33 = (s32[]{:T(128)}, f32[1,6,128]{2,1,0:T(8,128)S(1)}, f32[1,6,128]{2,1,0:T(8,128)S(1)}, f32[1,6,128,128]{3,2,1,0:T(8,128)S(1)}, s32[]{:T(128)}, /*index...) while((s32[]{:T(128)}, f32[1,6,128]{2,1,0:T(8,128)S(1)}, ...), condition=%wide.region_17.19_spmd, body=%wide.region_11.18_spmd.sunk | while | flops 827476224 | bytes 47396084 | solution.py:58
  80.8 3.6 %bitcast_reduce_fusion.5 = (f32[6,128,16]{1,0,2:T(8,128)S(1)}, f32[16,128,128,6]{2,1,3,0:T(8,128)}) fusion(bf16[128,1,6,128]{3,0,2,1:T(8,128)(2,1)S(1)} %get-tuple-element.525, bf16[16,128,1,128]{3,1,0,2:T(8,128)(2,1)S(1)} %get-tuple-element.524), kind=kOutput, calls=%fused_computation.32.clone.1 | convolution fusion | flops 405786624 | bytes 7061504 | tf_op jit(solution)/shard_map/while/body/qgjd,ckgd->gjqck/dot_general | solution.py:15
  84.5 0.8 add_compare_fusion.5
  85.4 4.7 %convert_reduce_fusion.5 = f32[6,128,16]{1,0,2:T(8,128)S(1)} fusion(f32[6,128,16]{1,0,2:T(8,128)S(1)} %get-tuple-element.491, f32[16,128,128,6]{2,1,3,0:T(8,128)} %get-tuple-element.492, pred[16]{0:T(512)(128)(4,1)S(1)} %add_compare_fusion.5), kind=kLoop, calls=%fused_computation.36.clone.1 | loop fusion | flops 9424896 | bytes 6389776 | tf_op jit(solution)/shard_map/while/body/reduce_sum | solution.py:23
  90.2 3.2 %fusion.59 = f32[6,128,128]{2,1,0:T(8,128)S(1)} fusion(f32[6,128,16]{1,0,2:T(8,128)S(1)} %get-tuple-element.494, bf16[16,128,1,128]{3,1,0,2:T(8,128)(2,1)S(1)} %get-tuple-element.526, f32[16,128,128,6]{2,1,3,0:T(8,128)S(1)} %copy-done, f32[6,128,16]{1,0,2:T(8,128)S(1)} %get-tuple-element.491, pred[16]{0:T(512)(128)(4,1)S(1)} %add_compare_fusion.5), kind=kOutput, calls=%fused_computation.30.clone.1 | convolution fusion | flops 411992064 | bytes 7307280 | tf_op jit(solution)/shard_map/while/body/gjqck,ckgd->gjqcd/dot_general | solution.py:24
  93.4 0.2 bitcast_add_fusion.11
  94.4 12.6 %while.32 = (s32[]{:T(128)}, f32[1,6,128]{2,1,0:T(8,128)S(1)}, f32[1,6,128]{2,1,0:T(8,128)S(1)}, f32[1,6,128,128]{3,2,1,0:T(8,128)S(1)}, s32[]{:T(128)}, /*index...) while((s32[]{:T(128)}, f32[1,6,128]{2,1,0:T(8,128)S(1)}, ...), condition=%wide.region_8.10_spmd, body=%wide.region_2.9_spmd.sunk | while | flops 827476224 | bytes 47396084 | solution.py:58
  94.4 3.6 %bitcast_reduce_fusion.4 = (f32[6,128,16]{1,0,2:T(8,128)S(1)}, f32[16,128,128,6]{2,1,3,0:T(8,128)}) fusion(bf16[128,1,6,128]{3,0,2,1:T(8,128)(2,1)S(1)} %get-tuple-element.558, bf16[16,128,1,128]{3,1,0,2:T(8,128)(2,1)S(1)} %get-tuple-element.557), kind=kOutput, calls=%fused_computation.7.clone.1 | convolution fusion | flops 405786624 | bytes 7061504 | tf_op jit(solution)/shard_map/while/body/qgjd,ckgd->gjqck/dot_general | solution.py:15
  98.1 0.7 add_compare_fusion.4
  98.9 4.5 %convert_reduce_fusion.4 = f32[6,128,16]{1,0,2:T(8,128)S(1)} fusion(f32[6,128,16]{1,0,2:T(8,128)S(1)} %get-tuple-element.474, f32[16,128,128,6]{2,1,3,0:T(8,128)} %get-tuple-element.475, pred[16]{0:T(512)(128)(4,1)S(1)} %add_compare_fusion.4), kind=kLoop, calls=%fused_computation.11.clone.1 | loop fusion | flops 9424896 | bytes 6389776 | tf_op jit(solution)/shard_map/while/body/reduce_sum | solution.py:23
  103.5 3.2 %fusion.54 = f32[6,128,128]{2,1,0:T(8,128)S(1)} fusion(f32[6,128,16]{1,0,2:T(8,128)S(1)} %get-tuple-element.477, bf16[16,128,1,128]{3,1,0,2:T(8,128)(2,1)S(1)} %get-tuple-element.559, f32[16,128,128,6]{2,1,3,0:T(8,128)S(1)} %copy-done.1, f32[6,128,16]{1,0,2:T(8,128)S(1)} %get-tuple-element.474, pred[16]{0:T(512)(128)(4,1)S(1)} %add_compare_fusion.4), kind=kOutput, calls=%fused_computation.5.clone.1 | convolution fusion | flops 411992064 | bytes 7307280 | tf_op jit(solution)/shard_map/while/body/gjqck,ckgd->gjqcd/dot_general | solution.py:24
  106.8 0.2 bitcast_add_fusion.9
  107.5 7.7 %fusion.32 = bf16[6144,256]{0,1:T(8,128)(2,1)} fusion(bf16[256,768]{1,0:T(8,128)(2,1)S(1)} %bitcast.214, bf16[768,6144]{1,0:T(8,128)(2,1)} %param.15), kind=kOutput, calls=%fused_computation.55 | convolution fusion | flops 2417491968 | bytes 12976128 | tf_op jit(solution)/shard_map/dot_general | solution.py:108
  115.2 39.2 %reduce-scatter.2.cloned.1.call-done = bf16[1536,256]{0,1:T(8,128)(2,1)} async-done(((bf16[6144,256]{0,1:T(8,128)(2,1)}), bf16[1536,256]{0,1:T(8,128)(2,1)}) %reduce-scatter.2.cloned.1.call-update) | async-done | bytes 786448 | tf_op jit(solution)/shard_map/reduce_scatter | solution.py:107
  (44 shorter events, 2.1 us)
Async XLA Ops:
  6.5 147.9 %reduce-scatter.2.cloned.1.call-start = ((), (), s32[]{:S(2)}) async-start(), calls=%async_computation.1 | async-start | bytes 3932160 | tf_op jit(solution)/shard_map/reduce_scatter | solution.py:107
  84.5 5.7 %copy-start = (f32[16,128,128,6]{2,1,3,0:T(8,128)S(1)}, f32[16,128,128,6]{2,1,3,0:T(8,128)}, u32[]{:S(2)}) copy-start(f32[16,128,128,6]{2,1,3,0:T(8,128)} %get-tuple-element.492) | copy-start | bytes 18874372 | tf_op jit(solution)/shard_map/while
  98.1 5.4 %copy-start.1 = (f32[16,128,128,6]{2,1,3,0:T(8,128)S(1)}, f32[16,128,128,6]{2,1,3,0:T(8,128)}, u32[]{:S(2)}) copy-start(f32[16,128,128,6]{2,1,3,0:T(8,128)} %get-tuple-element.475) | copy-start | bytes 18874372 | tf_op jit(solution)/shard_map/while
Sparse Core Ops, SparseCore 0:
  115.3 39.0 reduce-scatter.1
where the time goes:
time: 161 us
  blocking collectives  64.7 us (40%)
  waiting for transfers between devices  39.2 us (24%)
  matrix products  21.4 us (13%)
  other arithmetic  16 us (10%)
  between operations  14.9 us (9%)
  local copies, waits for them, and re-layouts  4.9 us (3%)
    reduce_scatter x1, waiting for transfers between devices, per_device(): lax.psum_scatter(lax.dot_general(out_weight, attention, (((0,), (1,)), ((...  39.2 us
    all_gather x1, blocking collectives, per_device(): lax.all_gather(value_rows, 'tok', axis=0, tiled=True)  33.3 us
    all_gather x1, blocking collectives, per_device(): lax.all_gather(key_rows, 'tok', axis=0, tiled=True)  31.4 us
    reduce_sum x2, other arithmetic, tile_block(): tile_sums = jnp.sum(prob_bf.astype(jnp.float32), axis=-1)  9.13 us
    dot_general x1, matrix products, per_device(): lax.dot_general(out_weight, attention, (((0,), (1,)), ((), ())), preferre...  7.67 us
    dot_general x2, matrix products, tile_block(): jnp.einsum('qgjd,ckgd->gjqck', query_tile, key_chosen, preferred_element_...  7.29 us
    dot_general x2, matrix products, tile_block(): jnp.einsum('gjqck,ckgd->gjqcd', prob_bf, value_chosen, preferred_element_...  6.43 us
  transfers between devices with their start and end apart: 1, of which 1 were waited for; matrix products, arithmetic and copies ran while one was open for 0% of the time, Pallas kernels for 0%

commit v1 on v0

--- a/solution.py
+++ b/solution.py
@@ -8,6 +8,13 @@
 TILE = 128
 NEGATIVE = -1e30
 tiles_per_turn = 16
+
+
+def swapped_in(x, axis, d):
+    count = lax.axis_size(axis)
+    parts = jnp.stack([x for _ in range(count)])
+    parts = lax.all_to_all(parts, axis, split_axis=0, concat_axis=0)
+    return jnp.concatenate(parts, axis=d)
 
 
 def tile_block(query_tile, key_chosen, value_chosen, shown_tiles, state, score_scale):
@@ -75,7 +82,7 @@
     initial = tuple(((empty_max, empty_sum, empty_out) for number in range(len(slot_rows))))
     every_key, every_value = (
         lax.all_gather(key_rows, "tok", axis=0, tiled=True),
-        lax.all_gather(value_rows, "tok", axis=0, tiled=True),
+        swapped_in(value_rows, "tok", 0),
     )
     tile_count = every_key.shape[0] // TILE
     key_tiles = every_key.reshape(tile_count, TILE, kv_local, HD)

time: 161 us -> 139 us (0.86)
  blocking collectives: 64.7 us -> 37.1 us
  starting transfers between devices: 0.01 us -> 7.32 us
  waiting for transfers between devices: 39.2 us -> 35.2 us
  local copies, waits for them, and re-layouts: 4.9 us -> 6.61 us
    all_gather x1 -> x0, blocking collectives: 33.3 us -> none  [per_device(): lax.all_gather(value_rows, 'tok', axis=0, tiled=True)]
    all_to_all x0 -> x1, starting transfers between devices: none -> 7.28 us  [swapped_in(): parts = lax.all_to_all(parts, axis, split_axis=0, concat_axis=0)]
    all_gather x1, blocking collectives: 31.4 us -> 37.1 us  [per_device(): lax.all_gather(key_rows, 'tok', axis=0, tiled=True)]
    reduce_scatter x1, waiting for transfers between devices: 39.2 us -> 35.2 us  [per_device(): lax.psum_scatter(lax.dot_general(out_weight, attention, (((0,), (1,)), ((...]
    another operation x2 -> x3, local copies, waits for them, and re-layouts: 0.01 us -> 1.7 us  [the longest x1 1.7 us: swapped_in(): parts = jnp.stack([x for _ in range(count)])]
  transfers between devices with their start and end apart: 1 -> 2, of which waited for: 1 -> 1; matrix products, arithmetic and copies ran while one was open for 0% -> 5% of each run, Pallas kernels for 0% -> 0%
where the time goes in v1:
time: 139 us
  blocking collectives  37.1 us (27%)
  waiting for transfers between devices  35.2 us (25%)
  matrix products  21.4 us (15%)
  other arithmetic  15.9 us (11%)
  between operations  14.9 us (11%)
  starting transfers between devices  7.32 us (5%)
  local copies, waits for them, and re-layouts  6.61 us (5%)
    all_gather x1, blocking collectives, per_device(): lax.all_gather(key_rows, 'tok', axis=0, tiled=True)  37.1 us
    reduce_scatter x1, waiting for transfers between devices, per_device(): lax.psum_scatter(lax.dot_general(out_weight, attention, (((0,), (1,)), ((...  35.2 us
    reduce_sum x2, other arithmetic, tile_block(): tile_sums = jnp.sum(prob_bf.astype(jnp.float32), axis=-1)  9.13 us
    dot_general x1, matrix products, per_device(): lax.dot_general(out_weight, attention, (((0,), (1,)), ((), ())), preferre...  7.66 us
    dot_general x2, matrix products, tile_block(): jnp.einsum('qgjd,ckgd->gjqck', query_tile, key_chosen, preferred_element_...  7.3 us
    all_to_all x1, starting transfers between devices, swapped_in(): parts = lax.all_to_all(parts, axis, split_axis=0, concat_axis=0)  7.28 us
    dot_general x2, matrix products, tile_block(): jnp.einsum('gjqck,ckgd->gjqcd', prob_bf, value_chosen, preferred_element_...  6.43 us
  transfers between devices with their start and end apart: 2, of which 1 were waited for; matrix products, arithmetic and copies ran while one was open for 5% of the time, Pallas kernels for 0%

profile of v1, /device:TPU:0, one launch (start us, length us, event | category | flops | bytes accessed | tf_op | source)
XLA Modules:
  0.0 138.6 jit_solution(1998146545819599603)
XLA Ops:
  6.5 1.7 %stack.4 = bf16[8,256,128]{2,1,0:T(8,128)(2,1)} broadcast(bf16[256,128]{1,0:T(8,128)(2,1)} %param.13), dimensions={1,2} | broadcast | bytes 589824 | tf_op jit(solution)/shard_map/stack | solution.py:15
  8.2 7.3 %all-to-all-start = ((bf16[8,256,128]{2,1,0:T(8,128)(2,1)}), bf16[8,256,128]{2,1,0:T(8,128)(2,1)S(1)}, u32[]{:S(2)}, u32[]{:S(2)}) async-start(bf16[8,256,128]{2,1,0:T(8,128)(2,1)} %stack.4), calls=%async_computation | async-start | bytes 1048576 | tf_op jit(solution)/shard_map/all_to_all | solution.py:16
  15.6 1.5 %subtract_bitcast_fusion.1 = (s32[16]{0:T(128)S(1)}, s32[16]{0:T(128)S(1)}, s32[]{:T(128)}, s32[]{:T(128)}) fusion(s32[2,16]{1,0:T(2,128)} %param.14), kind=kLoop, calls=%fused_computation.74 | loop fusion | flops 62 | bytes 264 | tf_op jit(solution)/shard_map/sub | solution.py:48
  17.0 37.1 %all_gather.3 = bf16[2048,128]{1,0:T(8,128)(2,1)S(1)} all-gather(bf16[256,128]{1,0:T(8,128)(2,1)} %param.12), channel_id=1, replica_groups=mesh['tok'=8,'head'=4] {'tok'}, dimensions={0}, use_global_device_ids=true | all-gather | bytes 589824 | tf_op jit(solution)/shard_map/all_gather | solution.py:84
  54.1 1.0 fusion.37
  55.2 1.3 sort.32
  58.1 0.6 gather_fusion.2
  58.8 1.3 sort.31
  60.1 0.6 gather_fusion
  61.1 0.6 gather_fusion.3
  61.8 0.6 gather_fusion.1
  62.6 12.8 %while.33 = (s32[]{:T(128)}, f32[1,6,128]{2,1,0:T(8,128)S(1)}, f32[1,6,128]{2,1,0:T(8,128)S(1)}, f32[1,6,128,128]{3,2,1,0:T(8,128)S(1)}, s32[]{:T(128)}, /*index...) while((s32[]{:T(128)}, f32[1,6,128]{2,1,0:T(8,128)S(1)}, ...), condition=%wide.region_17.19_spmd, body=%wide.region_11.18_spmd.sunk | while | flops 827476224 | bytes 47396084 | solution.py:65
  62.7 3.6 %bitcast_reduce_fusion.5 = (f32[6,128,16]{1,0,2:T(8,128)S(1)}, f32[16,128,128,6]{2,1,3,0:T(8,128)}) fusion(bf16[128,1,6,128]{3,0,2,1:T(8,128)(2,1)S(1)} %get-tuple-element.525, bf16[16,128,1,128]{3,1,0,2:T(8,128)(2,1)S(1)} %get-tuple-element.524), kind=kOutput, calls=%fused_computation.32.clone.1 | convolution fusion | flops 405786624 | bytes 7061504 | tf_op jit(solution)/shard_map/while/body/qgjd,ckgd->gjqck/dot_general | solution.py:22
  66.3 0.8 add_compare_fusion.5
  67.2 4.7 %convert_reduce_fusion.5 = f32[6,128,16]{1,0,2:T(8,128)S(1)} fusion(f32[6,128,16]{1,0,2:T(8,128)S(1)} %get-tuple-element.491, f32[16,128,128,6]{2,1,3,0:T(8,128)} %get-tuple-element.492, pred[16]{0:T(512)(128)(4,1)S(1)} %add_compare_fusion.5), kind=kLoop, calls=%fused_computation.36.clone.1 | loop fusion | flops 9424896 | bytes 6389776 | tf_op jit(solution)/shard_map/while/body/reduce_sum | solution.py:30
  72.0 3.2 %fusion.59 = f32[6,128,128]{2,1,0:T(8,128)S(1)} fusion(f32[6,128,16]{1,0,2:T(8,128)S(1)} %get-tuple-element.494, bf16[16,128,1,128]{3,1,0,2:T(8,128)(2,1)S(1)} %get-tuple-element.526, f32[16,128,128,6]{2,1,3,0:T(8,128)S(1)} %copy-done, f32[6,128,16]{1,0,2:T(8,128)S(1)} %get-tuple-element.491, pred[16]{0:T(512)(128)(4,1)S(1)} %add_compare_fusion.5), kind=kOutput, calls=%fused_computation.30.clone.1 | convolution fusion | flops 411992064 | bytes 7307280 | tf_op jit(solution)/shard_map/while/body/gjqck,ckgd->gjqcd/dot_general | solution.py:31
  75.8 12.6 %while.32 = (s32[]{:T(128)}, f32[1,6,128]{2,1,0:T(8,128)S(1)}, f32[1,6,128]{2,1,0:T(8,128)S(1)}, f32[1,6,128,128]{3,2,1,0:T(8,128)S(1)}, s32[]{:T(128)}, /*index...) while((s32[]{:T(128)}, f32[1,6,128]{2,1,0:T(8,128)S(1)}, ...), condition=%wide.region_8.10_spmd, body=%wide.region_2.9_spmd.sunk | while | flops 827476224 | bytes 47396084 | solution.py:65
  75.9 3.7 %bitcast_reduce_fusion.4 = (f32[6,128,16]{1,0,2:T(8,128)S(1)}, f32[16,128,128,6]{2,1,3,0:T(8,128)}) fusion(bf16[128,1,6,128]{3,0,2,1:T(8,128)(2,1)S(1)} %get-tuple-element.558, bf16[16,128,1,128]{3,1,0,2:T(8,128)(2,1)S(1)} %get-tuple-element.557), kind=kOutput, calls=%fused_computation.7.clone.1 | convolution fusion | flops 405786624 | bytes 7061504 | tf_op jit(solution)/shard_map/while/body/qgjd,ckgd->gjqck/dot_general | solution.py:22
  79.5 0.7 add_compare_fusion.4
  80.3 4.5 %convert_reduce_fusion.4 = f32[6,128,16]{1,0,2:T(8,128)S(1)} fusion(f32[6,128,16]{1,0,2:T(8,128)S(1)} %get-tuple-element.474, f32[16,128,128,6]{2,1,3,0:T(8,128)} %get-tuple-element.475, pred[16]{0:T(512)(128)(4,1)S(1)} %add_compare_fusion.4), kind=kLoop, calls=%fused_computation.11.clone.1 | loop fusion | flops 9424896 | bytes 6389776 | tf_op jit(solution)/shard_map/while/body/reduce_sum | solution.py:30
  85.0 3.2 %fusion.54 = f32[6,128,128]{2,1,0:T(8,128)S(1)} fusion(f32[6,128,16]{1,0,2:T(8,128)S(1)} %get-tuple-element.477, bf16[16,128,1,128]{3,1,0,2:T(8,128)(2,1)S(1)} %get-tuple-element.559, f32[16,128,128,6]{2,1,3,0:T(8,128)S(1)} %copy-done.1, f32[6,128,16]{1,0,2:T(8,128)S(1)} %get-tuple-element.474, pred[16]{0:T(512)(128)(4,1)S(1)} %add_compare_fusion.4), kind=kOutput, calls=%fused_computation.5.clone.1 | convolution fusion | flops 411992064 | bytes 7307280 | tf_op jit(solution)/shard_map/while/body/gjqck,ckgd->gjqcd/dot_general | solution.py:31
  88.2 0.2 bitcast_add_fusion.9
  88.9 7.7 %fusion.32 = bf16[6144,256]{0,1:T(8,128)(2,1)} fusion(bf16[256,768]{1,0:T(8,128)(2,1)S(1)} %bitcast.214, bf16[768,6144]{1,0:T(8,128)(2,1)} %param.15), kind=kOutput, calls=%fused_computation.55 | convolution fusion | flops 2417491968 | bytes 12976128 | tf_op jit(solution)/shard_map/dot_general | solution.py:115
  96.6 35.2 %reduce-scatter.2.cloned.1.call-done = bf16[1536,256]{0,1:T(8,128)(2,1)} async-done(((bf16[6144,256]{0,1:T(8,128)(2,1)}), bf16[1536,256]{0,1:T(8,128)(2,1)}) %reduce-scatter.2.cloned.1.call-update) | async-done | bytes 786448 | tf_op jit(solution)/shard_map/reduce_scatter | solution.py:114
  (46 shorter events, 2.4 us)
Async XLA Ops:
  8.2 52.9 %all-to-all-start = ((bf16[8,256,128]{2,1,0:T(8,128)(2,1)}), bf16[8,256,128]{2,1,0:T(8,128)(2,1)S(1)}, u32[]{:S(2)}, u32[]{:S(2)}) async-start(bf16[8,256,128]{2,1,0:T(8,128)(2,1)} %stack.4), calls=%async_computation | async-start | bytes 1048576 | tf_op jit(solution)/shard_map/all_to_all | solution.py:16
  15.5 116.3 %reduce-scatter.2.cloned.1.call-start = ((), (), s32[]{:S(2)}) async-start(), calls=%async_computation.2 | async-start | bytes 3932160 | tf_op jit(solution)/shard_map/reduce_scatter | solution.py:114
  66.3 5.7 %copy-start = (f32[16,128,128,6]{2,1,3,0:T(8,128)S(1)}, f32[16,128,128,6]{2,1,3,0:T(8,128)}, u32[]{:S(2)}) copy-start(f32[16,128,128,6]{2,1,3,0:T(8,128)} %get-tuple-element.492) | copy-start | bytes 18874372 | tf_op jit(solution)/shard_map/while
  79.5 5.4 %copy-start.1 = (f32[16,128,128,6]{2,1,3,0:T(8,128)S(1)}, f32[16,128,128,6]{2,1,3,0:T(8,128)}, u32[]{:S(2)}) copy-start(f32[16,128,128,6]{2,1,3,0:T(8,128)} %get-tuple-element.475) | copy-start | bytes 18874372 | tf_op jit(solution)/shard_map/while
Sparse Core Ops, SparseCore 0:
  96.7 35.0 reduce-scatter.1
